TPU v7x, 32 devices: a whole 2x2x4 slice. The times are simulated.
32 devices in a mesh: groups: 2 (over y), ctx: 8 (over z, x), head: 2 (over core).
Axes of the slice: x: 2, y: 2, z: 4, core: 2. Of those that a mesh axis runs over, the one named last changes fastest.
Arguments:
- keys_values: bfloat16 [2, 8192, 1024], P(None, ('groups', 'ctx'), 'head'), parts along dimension 1, may hold values from -6 to 6
- span_order: int32 [32], P('groups'), parts along dimension 0, may hold values from 0 to 15, as said below
- page_table: int32 [64], P('groups'), parts along dimension 0, may hold values from 0 to 31, as said below
Outputs:
- paged_cache: bfloat16 [2, 64, 128, 1024], P(None, ('groups', 'ctx', 'head')), parts along dimension 1
There are 2 independent parts, one for each index of `groups`. A program takes and returns all parts, laid end to end along the dimension named above; each array names one. Nothing has to cross between parts.
Inputs may be any that keep to these rules, and one draw needn't show every extreme that they name: `span_order`: blocks 2 c and 2 c + 1 hold two spans whose numbers add to 15; every span is held once. A permutation of the slots in which page p goes to a slot of p // 2, that is page_table[p] // 2 == p // 2.
All inputs are finite; a program needn't handle non-finite values.
Results may differ from a plain program's by a relative error of at most 0.001.
Values may be sent and summed in bfloat16 or wider, within the bound.
No kernel may reach another device: no remote copies, remote signals or barrier semaphores. Data moves between devices by JAX's collectives and lax.ppermute only.
A program may use at most 64 MiB of HBM per device.

v0:
```python
import functools

import jax
import jax.numpy as jnp
from jax import lax
from jax.experimental import pallas as pl
from jax.experimental.pallas import tpu as pltpu
from jax.sharding import PartitionSpec as P

PAGE = 128
SUBLANES = 16
AXES = ("ctx", "head")
VMEM = pl.BlockSpec(memory_space=pltpu.VMEM)
SMEM = pl.BlockSpec(memory_space=pltpu.SMEM)
SMALL = pltpu.CompilerParams(vmem_limit_bytes=8 << 20)
HBM = pl.BlockSpec(memory_space=pltpu.HBM)


def swap(x, distance, size):
    return lax.ppermute(x, AXES, [(i, i ^ distance) for i in range(size)])


def prepare(chips, piece, spans, data, *refs):
    outs, table, table_sem, sems = refs[:-3], *refs[-3:]
    near = chips // 2
    me = lax.axis_index("ctx")
    load = pltpu.make_async_copy(spans, table, table_sem)
    load.start()
    load.wait()
    mine_low = me < near
    first_low = table[2 * me] < chips
    stay = jnp.where(mine_low == first_low, 0, 1)
    rows = near * piece
    copies = []

    def piece_at(block, target):
        start = block * rows + lax.rem(target, near) * piece
        return pl.ds(pl.multiple_of(start, piece), piece)

    n = 0
    for kind in range(2):
        for d in range(near, chips):
            src = data.at[kind, piece_at(1 - stay, me ^ d), :]
            copies.append(pltpu.make_async_copy(src, outs[n], sems.at[n]))
            n += 1
    for d in range(near):
        src = data.at[:, piece_at(stay, me ^ d), :]
        copies.append(pltpu.make_async_copy(src, outs[n], sems.at[n]))
        n += 1
    for copy in copies:
        copy.start()
    for copy in copies:
        copy.wait()


def route(chips, kind, spans, *refs):
    near = chips // 2
    ins, outs = refs[:chips], refs[chips:]
    me = lax.axis_index("ctx")
    local = lax.rem(me, near)
    low = me < near
    for d in range(chips):
        source = me ^ d
        a, b = spans[2 * source], spans[2 * source + 1]
        span = jnp.where((a < chips) == low, a, b)
        parity = lax.rem(span, 2)
        distance = lax.rem(span // 2, near) ^ local
        for j in range(near):

            @pl.when(distance == j)
            def _(d=d, j=j):
                outs[j][parity] = ins[d][kind] if d < near else ins[d][...]


def hand_over(near, *refs):
    ins, out = refs[:near], refs[near]
    other = 1 - lax.axis_index("head")
    for j in range(near):
        out[j] = ins[j][other]


def finish(near, piece, table, *refs):
    per_span = near * piece // PAGE
    own = [refs[:near], refs[near : 2 * near]]
    got = refs[2 * near : 2 * near + 2]
    out, sems = refs[2 * near + 2 :]
    me = lax.axis_index("ctx")
    head = lax.axis_index("head")
    width = out.shape[3] // 2
    device = 2 * me + head
    local = lax.rem(me, near)
    copies = []
    for kind in range(2):
        for j in range(near):
            row = (local ^ j) * piece
            slot = table[device * per_span + row // PAGE] - device * per_span
            rows = pl.ds(pl.multiple_of(lax.rem(row, PAGE), piece), piece)
            for src, side in ((own[kind][j].at[head], head), (got[kind].at[j], 1 - head)):
                cols = pl.ds(pl.multiple_of(side * width, width), width)
                dst = out.at[kind, slot, rows, cols]
                copies.append(pltpu.make_async_copy(src, dst, sems.at[len(copies)]))
    for copy in copies:
        copy.start()
    for copy in copies:
        copy.wait()


def by_permutes(keys_values, span_order, page_table):
    chips = lax.axis_size("ctx")
    size = 2 * chips
    near = chips // 2
    width = keys_values.shape[2]
    span_len = keys_values.shape[1] // 2
    piece = span_len // near
    dtype = keys_values.dtype
    one = jax.ShapeDtypeStruct((piece, width), dtype)
    two = jax.ShapeDtypeStruct((2, piece, width), dtype)
    n = 2 * near + near
    pieces = pl.pallas_call(
        functools.partial(prepare, chips, piece),
        out_shape=[one] * (2 * near) + [two] * near,
        in_specs=[HBM, HBM],
        out_specs=[VMEM] * n,
        scratch_shapes=[
            pltpu.SMEM(span_order.shape, span_order.dtype),
            pltpu.SemaphoreType.DMA,
            pltpu.SemaphoreType.DMA((n,)),
        ],
        name="prepare",
            compiler_params=SMALL,
    )(
        pltpu.with_memory_space_constraint(span_order, pltpu.HBM),
        pltpu.with_memory_space_constraint(keys_values, pltpu.HBM),
    )
    far = [
        [swap(pieces[kind * near + i], 2 * (near + i), size) for i in range(near)]
        for kind in range(2)
    ]
    stay = [pieces[2 * near]] + [
        swap(pieces[2 * near + d], 2 * d, size) for d in range(1, near)
    ]
    own, got = [], []
    for kind in range(2):
        routed = pl.pallas_call(
            functools.partial(route, chips, kind),
            out_shape=[two] * near,
            in_specs=[SMEM] + [VMEM] * chips,
            out_specs=[VMEM] * near,
            name="route",
            compiler_params=SMALL,
        )(span_order, *stay, *far[kind])
        held = [routed[0]] + [swap(routed[j], 2 * j, size) for j in range(1, near)]
        send = pl.pallas_call(
            functools.partial(hand_over, near),
            out_shape=jax.ShapeDtypeStruct((near, piece, width), dtype),
            in_specs=[VMEM] * near,
            out_specs=VMEM,
            name="hand_over",
            compiler_params=SMALL,
        )(*held)
        own += held
        got.append(swap(send, 1, size))
    return pl.pallas_call(
        functools.partial(finish, near, piece),
        out_shape=jax.ShapeDtypeStruct((2, span_len // PAGE, PAGE, 2 * width), dtype),
        in_specs=[SMEM] + [VMEM] * (2 * near + 2),
        out_specs=HBM,
        scratch_shapes=[pltpu.SemaphoreType.DMA((4 * near,))],
        name="finish",
            compiler_params=SMALL,
    )(page_table, *own, *got)


def by_all_to_alls(keys_values, span_order, page_table):
    tok_rows = keys_values.shape[1]
    width = keys_values.shape[2]
    span_len = tok_rows // 2
    per_span = span_len // PAGE
    ctx_index = lax.axis_index("ctx")
    spans = lax.axis_size("ctx") * lax.axis_size("head")
    half = spans // 2
    piece = span_len // half

    first_span = lax.dynamic_index_in_dim(span_order, 2 * ctx_index, keepdims=False)
    flip = first_span >= half
    blocks = keys_values.reshape(2, 2, half, piece, width)
    low = jnp.where(flip, blocks[:, 1], blocks[:, 0])
    high = jnp.where(flip, blocks[:, 0], blocks[:, 1])
    spread = jnp.stack([low, high], axis=0).transpose(0, 2, 1, 3, 4)
    spread = spread.reshape(spans, 2, piece, width)
    spread = lax.all_to_all(spread, AXES, split_axis=0, concat_axis=0, tiled=True)

    device = 2 * ctx_index + lax.axis_index("head")
    base = (device // half) * half
    wanted = base + jnp.arange(half, dtype=jnp.int32)
    chips = jnp.arange(spans, dtype=jnp.int32) // 2
    holder = jnp.sum(jnp.where(span_order[None, :] == wanted[:, None], chips[None, :], 0), axis=1)
    spread = spread.reshape(half, 2, 2, piece, width)
    routed = jnp.take(spread, holder, axis=0, mode="clip")
    groups = [list(range(half)), list(range(half, spans))]
    routed = lax.all_to_all(
        routed, AXES, split_axis=0, concat_axis=0, tiled=True, axis_index_groups=groups
    )
    rows = routed.transpose(2, 0, 3, 1, 4).reshape(2, per_span, PAGE, 2 * width)
    slots = lax.dynamic_slice_in_dim(page_table, device * per_span, per_span) - device * per_span
    order = jnp.sum(
        jnp.where(
            slots[None, :] == jnp.arange(per_span, dtype=jnp.int32)[:, None],
            jnp.arange(per_span, dtype=jnp.int32)[None, :],
            0,
        ),
        axis=1,
    )
    return jnp.take(rows, order, axis=1, mode="clip")


def per_device(keys_values, span_order, page_table):
    chips = lax.axis_size("ctx")
    piece = keys_values.shape[1] // chips
    whole_tiles = piece % SUBLANES == 0 and PAGE % piece == 0
    if chips & (chips - 1) == 0 and whole_tiles:
        return by_permutes(keys_values, span_order, page_table)
    return by_all_to_alls(keys_values, span_order, page_table)


def solution(mesh):
    in_specs = (P(None, ("groups", "ctx"), "head"), P("groups"), P("groups"))
    out_specs = P(None, ("groups", "ctx", "head"), None, None)
    return jax.shard_map(
        per_device, mesh=mesh, in_specs=in_specs, out_specs=out_specs, check_vma=False
    )
```

profile of v0, /device:TPU:0, one launch (start us, length us, event | category | flops | bytes accessed | tf_op | source)
XLA Modules:
  0.0 50.7 jit_solution(14678018877300469979)
XLA Ops:
  0.0 2.1 %prepare.1 = (bf16[64,512]{1,0:T(8,128)(2,1)S(1)}, bf16[64,512]{1,0:T(8,128)(2,1)S(1)}, bf16[64,512]{1,0:T(8,128)(2,1)S(1)}, bf16[64,512]{1,0:T(8,128)(2,1)S(1)}...) custom-call(s32[16]{0:T(128)} %spans.5, ...), custom_call_target="tpu_custom_call" | custom-call | tf_op jit(solution)/shard_map/prepare/pallas_call | solution.py:119
  2.1 4.1 %collective-permute-start.10 = (bf16[64,512]{1,0:T(8,128)(2,1)S(1)}, bf16[64,512]{1,0:T(8,128)(2,1)S(1)}, u32[]{:S(2)}, u32[]{:S(2)}) collective-permute-start(bf16[64,512]{1,0:T(8,128)(2,1)S(1)} %get-tuple-element.37), channel_id=1, source_target_pairs={{0,8},{1,9},{2,10},{3,11},{4,12},{5,13},{6,14},{7,15},{8,0},{9,1},... | collective-permute-start | bytes 196616 | tf_op jit(solution)/shard_map/ppermute | solution.py:20
  6.2 1.3 %collective-permute-start.11 = (bf16[64,512]{1,0:T(8,128)(2,1)S(1)}, bf16[64,512]{1,0:T(8,128)(2,1)S(1)}, u32[]{:S(2)}, u32[]{:S(2)}) collective-permute-start(bf16[64,512]{1,0:T(8,128)(2,1)S(1)} %get-tuple-element.38), channel_id=1, source_target_pairs={{0,10},{1,11},{2,8},{3,9},{4,14},{5,15},{6,12},{7,13},{8,2},{9,3},... | collective-permute-start | bytes 196616 | tf_op jit(solution)/shard_map/ppermute | solution.py:20
  7.5 0.3 collective-permute-start
  7.8 1.8 %collective-permute-start.1 = (bf16[2,64,512]{2,1,0:T(8,128)(2,1)S(1)}, bf16[2,64,512]{2,1,0:T(8,128)(2,1)S(1)}, u32[]{:S(2)}, u32[]{:S(2)}) collective-permute-start(bf16[2,64,512]{2,1,0:T(8,128)(2,1)S(1)} %get-tuple-element.27), channel_id=1, source_target_pairs={{0,4},{1,5},{2,6},{3,7},{4,0},{5,1},{6,2},{7,3},{8,12},{9,13},{10,... | collective-permute-start | bytes 393224 | tf_op jit(solution)/shard_map/ppermute | solution.py:20
  9.6 1.4 %collective-permute-start.2 = (bf16[2,64,512]{2,1,0:T(8,128)(2,1)S(1)}, bf16[2,64,512]{2,1,0:T(8,128)(2,1)S(1)}, u32[]{:S(2)}, u32[]{:S(2)}) collective-permute-start(bf16[2,64,512]{2,1,0:T(8,128)(2,1)S(1)} %get-tuple-element.28), channel_id=1, source_target_pairs={{0,6},{1,7},{2,4},{3,5},{4,2},{5,3},{6,0},{7,1},{8,14},{9,15},{10,... | collective-permute-start | bytes 393224 | tf_op jit(solution)/shard_map/ppermute | solution.py:20
  11.0 0.0 collective-permute-done.10.refs_4_
  11.0 4.1 %collective-permute-start.12 = (bf16[64,512]{1,0:T(8,128)(2,1)S(1)}, bf16[64,512]{1,0:T(8,128)(2,1)S(1)}, u32[]{:S(2)}, u32[]{:S(2)}) collective-permute-start(bf16[64,512]{1,0:T(8,128)(2,1)S(1)} %get-tuple-element.39), channel_id=1, source_target_pairs={{0,12},{1,13},{2,14},{3,15},{4,8},{5,9},{6,10},{7,11},{8,4},{9,5},... | collective-permute-start | bytes 196616 | tf_op jit(solution)/shard_map/ppermute | solution.py:20
  15.1 0.0 collective-permute-done.11.refs_5_
  15.1 0.0 copy-start
  15.1 2.2 %collective-permute-start.13 = (bf16[64,512]{1,0:T(8,128)(2,1)S(1)}, bf16[64,512]{1,0:T(8,128)(2,1)S(1)}, u32[]{:S(2)}, u32[]{:S(2)}) collective-permute-start(bf16[64,512]{1,0:T(8,128)(2,1)S(1)} %get-tuple-element.40), channel_id=1, source_target_pairs={{0,14},{1,15},{2,12},{3,13},{4,10},{5,11},{6,8},{7,9},{8,6},{9,7},... | collective-permute-start | bytes 196616 | tf_op jit(solution)/shard_map/ppermute | solution.py:20
  17.3 2.4 %collective-permute-done.12.refs_6_ = bf16[64,512]{1,0:T(8,128)(2,1)S(1)} collective-permute-done((bf16[64,512]{1,0:T(8,128)(2,1)S(1)}, bf16[64,512]{1,0:T(8,128)(2,1)S(1)}, u32[]{:S(2)}, u32[]{:S(2)}) %collective-permute-start.12) | collective-permute-done | bytes 65568 | tf_op jit(solution)/shard_map/ppermute | solution.py:20
  19.7 2.3 %collective-permute-done.13.refs_7_ = bf16[64,512]{1,0:T(8,128)(2,1)S(1)} collective-permute-done((bf16[64,512]{1,0:T(8,128)(2,1)S(1)}, bf16[64,512]{1,0:T(8,128)(2,1)S(1)}, u32[]{:S(2)}, u32[]{:S(2)}) %collective-permute-start.13) | collective-permute-done | bytes 65568 | tf_op jit(solution)/shard_map/ppermute | solution.py:20
  22.0 0.0 collective-permute-done.refs_1_
  22.0 0.0 collective-permute-done.1.refs_2_
  22.0 0.0 collective-permute-done.2.refs_3_
  22.0 0.0 copy-done
  22.1 0.9 %route.3 = (bf16[2,64,512]{2,1,0:T(8,128)(2,1)S(1)}, bf16[2,64,512]{2,1,0:T(8,128)(2,1)S(1)}, bf16[2,64,512]{2,1,0:T(8,128)(2,1)S(1)}, bf16[2,64,512]{2,1,0:T(8,128)(2,1)S(1)}) custom-call(s32[16]{0:T(128)S(1)} %copy-done, bf16[2,64,512]{2,1,0:T(8,128)(2,1)S(1)} %get-tuple-element.25.refs_0_, bf16[2,64,512]{2,1,0:T(8,128)(2,1)S(1)} %collective-permute-done.refs_1_, ...), custom_call_target="tpu_custom_call" | custom-call | tf_op jit(solution)/shard_map/route/pallas_call | solution.py:144
  22.9 1.3 %collective-permute-start.14 = (bf16[2,64,512]{2,1,0:T(8,128)(2,1)S(1)}, bf16[2,64,512]{2,1,0:T(8,128)(2,1)S(1)}, u32[]{:S(2)}, u32[]{:S(2)}) collective-permute-start(bf16[2,64,512]{2,1,0:T(8,128)(2,1)S(1)} %get-tuple-element.42), channel_id=1, source_target_pairs={{0,2},{1,3},{2,0},{3,1},{4,6},{5,7},{6,4},{7,5},{8,10},{9,11},{10,... | collective-permute-start | bytes 393224 | tf_op jit(solution)/shard_map/ppermute | solution.py:20
  24.3 0.5 %collective-permute-start.3 = (bf16[64,512]{1,0:T(8,128)(2,1)S(1)}, bf16[64,512]{1,0:T(8,128)(2,1)S(1)}, u32[]{:S(2)}, u32[]{:S(2)}) collective-permute-start(bf16[64,512]{1,0:T(8,128)(2,1)S(1)} %get-tuple-element.29), channel_id=1, source_target_pairs={{0,8},{1,9},{2,10},{3,11},{4,12},{5,13},{6,14},{7,15},{8,0},{9,1},... | collective-permute-start | bytes 196616 | tf_op jit(solution)/shard_map/ppermute | solution.py:20
  24.8 2.6 %collective-permute-start.4 = (bf16[64,512]{1,0:T(8,128)(2,1)S(1)}, bf16[64,512]{1,0:T(8,128)(2,1)S(1)}, u32[]{:S(2)}, u32[]{:S(2)}) collective-permute-start(bf16[64,512]{1,0:T(8,128)(2,1)S(1)} %get-tuple-element.30), channel_id=1, source_target_pairs={{0,10},{1,11},{2,8},{3,9},{4,14},{5,15},{6,12},{7,13},{8,2},{9,3},... | collective-permute-start | bytes 196616 | tf_op jit(solution)/shard_map/ppermute | solution.py:20
  27.4 3.2 %collective-permute-start.5 = (bf16[64,512]{1,0:T(8,128)(2,1)S(1)}, bf16[64,512]{1,0:T(8,128)(2,1)S(1)}, u32[]{:S(2)}, u32[]{:S(2)}) collective-permute-start(bf16[64,512]{1,0:T(8,128)(2,1)S(1)} %get-tuple-element.31), channel_id=1, source_target_pairs={{0,12},{1,13},{2,14},{3,15},{4,8},{5,9},{6,10},{7,11},{8,4},{9,5},... | collective-permute-start | bytes 196616 | tf_op jit(solution)/shard_map/ppermute | solution.py:20
  30.5 1.4 %collective-permute-start.6 = (bf16[64,512]{1,0:T(8,128)(2,1)S(1)}, bf16[64,512]{1,0:T(8,128)(2,1)S(1)}, u32[]{:S(2)}, u32[]{:S(2)}) collective-permute-start(bf16[64,512]{1,0:T(8,128)(2,1)S(1)} %get-tuple-element.32), channel_id=1, source_target_pairs={{0,14},{1,15},{2,12},{3,13},{4,10},{5,11},{6,8},{7,9},{8,6},{9,7},... | collective-permute-start | bytes 196616 | tf_op jit(solution)/shard_map/ppermute | solution.py:20
  31.9 0.0 collective-permute-done.3.refs_4_
  31.9 0.0 collective-permute-start.15
  31.9 4.0 %collective-permute-done.4.refs_5_ = bf16[64,512]{1,0:T(8,128)(2,1)S(1)} collective-permute-done((bf16[64,512]{1,0:T(8,128)(2,1)S(1)}, bf16[64,512]{1,0:T(8,128)(2,1)S(1)}, u32[]{:S(2)}, u32[]{:S(2)}) %collective-permute-start.4) | collective-permute-done | bytes 65568 | tf_op jit(solution)/shard_map/ppermute | solution.py:20
  35.9 0.0 collective-permute-start.16
  35.9 0.0 collective-permute-done.5.refs_6_
  35.9 1.8 %collective-permute-done.6.refs_7_ = bf16[64,512]{1,0:T(8,128)(2,1)S(1)} collective-permute-done((bf16[64,512]{1,0:T(8,128)(2,1)S(1)}, bf16[64,512]{1,0:T(8,128)(2,1)S(1)}, u32[]{:S(2)}, u32[]{:S(2)}) %collective-permute-start.6) | collective-permute-done | bytes 65568 | tf_op jit(solution)/shard_map/ppermute | solution.py:20
  37.7 0.9 %route.2 = (bf16[2,64,512]{2,1,0:T(8,128)(2,1)S(1)}, bf16[2,64,512]{2,1,0:T(8,128)(2,1)S(1)}, bf16[2,64,512]{2,1,0:T(8,128)(2,1)S(1)}, bf16[2,64,512]{2,1,0:T(8,128)(2,1)S(1)}) custom-call(s32[16]{0:T(128)S(1)} %copy-done, bf16[2,64,512]{2,1,0:T(8,128)(2,1)S(1)} %get-tuple-element.25.refs_0_, bf16[2,64,512]{2,1,0:T(8,128)(2,1)S(1)} %collective-permute-done.refs_1_, ...), custom_call_target="tpu_custom_call" | custom-call | tf_op jit(solution)/shard_map/route/pallas_call | solution.py:144
  38.6 0.4 collective-permute-start.7
  39.0 1.8 %collective-permute-start.8 = (bf16[2,64,512]{2,1,0:T(8,128)(2,1)S(1)}, bf16[2,64,512]{2,1,0:T(8,128)(2,1)S(1)}, u32[]{:S(2)}, u32[]{:S(2)}) collective-permute-start(bf16[2,64,512]{2,1,0:T(8,128)(2,1)S(1)} %get-tuple-element.35), channel_id=1, source_target_pairs={{0,4},{1,5},{2,6},{3,7},{4,0},{5,1},{6,2},{7,3},{8,12},{9,13},{10,... | collective-permute-start | bytes 393224 | tf_op jit(solution)/shard_map/ppermute | solution.py:20
  40.8 0.0 collective-permute-done.14.refs_1_.refs_5_
  40.8 1.3 %collective-permute-start.9 = (bf16[2,64,512]{2,1,0:T(8,128)(2,1)S(1)}, bf16[2,64,512]{2,1,0:T(8,128)(2,1)S(1)}, u32[]{:S(2)}, u32[]{:S(2)}) collective-permute-start(bf16[2,64,512]{2,1,0:T(8,128)(2,1)S(1)} %get-tuple-element.36), channel_id=1, source_target_pairs={{0,6},{1,7},{2,4},{3,5},{4,2},{5,3},{6,0},{7,1},{8,14},{9,15},{10,... | collective-permute-start | bytes 393224 | tf_op jit(solution)/shard_map/ppermute | solution.py:20
  42.1 0.0 collective-permute-done.15.refs_2_.refs_6_
  42.1 0.5 %collective-permute-done.16.refs_3_.refs_7_ = bf16[2,64,512]{2,1,0:T(8,128)(2,1)S(1)} collective-permute-done((bf16[2,64,512]{2,1,0:T(8,128)(2,1)S(1)}, bf16[2,64,512]{2,1,0:T(8,128)(2,1)S(1)}, u32[]{:S(2)}, u32[]{:S(2)}) %collective-permute-start.16) | collective-permute-done | bytes 131104 | tf_op jit(solution)/shard_map/ppermute | solution.py:20
  42.7 0.1 collective-permute-start.18
  42.8 2.2 %collective-permute-done.7.refs_1_ = bf16[2,64,512]{2,1,0:T(8,128)(2,1)S(1)} collective-permute-done((bf16[2,64,512]{2,1,0:T(8,128)(2,1)S(1)}, bf16[2,64,512]{2,1,0:T(8,128)(2,1)S(1)}, u32[]{:S(2)}, u32[]{:S(2)}) %collective-permute-start.7) | collective-permute-done | bytes 131104 | tf_op jit(solution)/shard_map/ppermute | solution.py:20
  45.0 0.2 collective-permute-done.8.refs_2_
  45.2 2.2 %collective-permute-done.9.refs_3_ = bf16[2,64,512]{2,1,0:T(8,128)(2,1)S(1)} collective-permute-done((bf16[2,64,512]{2,1,0:T(8,128)(2,1)S(1)}, bf16[2,64,512]{2,1,0:T(8,128)(2,1)S(1)}, u32[]{:S(2)}, u32[]{:S(2)}) %collective-permute-start.9) | collective-permute-done | bytes 131104 | tf_op jit(solution)/shard_map/ppermute | solution.py:20
  47.4 0.0 copy-start.1
  47.4 0.1 collective-permute-start.17
  47.5 0.0 collective-permute-done.18.refs_9_
  47.5 1.5 %collective-permute-done.17.refs_8_ = bf16[4,64,512]{2,1,0:T(8,128)(2,1)S(1)} collective-permute-done((bf16[4,64,512]{2,1,0:T(8,128)(2,1)S(1)}, bf16[4,64,512]{2,1,0:T(8,128)(2,1)S(1)}, u32[]{:S(2)}, u32[]{:S(2)}) %collective-permute-start.17) | collective-permute-done | bytes 262176 | tf_op jit(solution)/shard_map/ppermute | solution.py:20
  49.0 0.0 copy-done.1
  49.0 1.7 %finish.1 = bf16[2,2,128,1024]{3,2,1,0:T(8,128)(2,1)} custom-call(s32[32]{0:T(128)S(1)} %copy-done.1, bf16[2,64,512]{2,1,0:T(8,128)(2,1)S(1)} %get-tuple-element.33.refs_0_, bf16[2,64,512]{2,1,0:T(8,128)(2,1)S(1)} %collective-permute-done.7.refs_1_, bf16[2,64,512]{2,1,0:T(8,128)(2,1)S(1)} %collective-permute-done.8.refs_2_, ...), custom_call_target="tpu_custom_call" | custom-call | tf_op jit(solution)/shard_map/finish/pallas_call | solution.py:163
  (2 shorter events, 0.0 us)
Async XLA Ops:
  2.1 8.9 %collective-permute-start.10 = (bf16[64,512]{1,0:T(8,128)(2,1)S(1)}, bf16[64,512]{1,0:T(8,128)(2,1)S(1)}, u32[]{:S(2)}, u32[]{:S(2)}) collective-permute-start(bf16[64,512]{1,0:T(8,128)(2,1)S(1)} %get-tuple-element.37), channel_id=1, source_target_pairs={{0,8},{1,9},{2,10},{3,11},{4,12},{5,13},{6,14},{7,15},{8,0},{9,1},... | collective-permute-start | bytes 196616 | tf_op jit(solution)/shard_map/ppermute | solution.py:20
  6.2 8.8 %collective-permute-start.11 = (bf16[64,512]{1,0:T(8,128)(2,1)S(1)}, bf16[64,512]{1,0:T(8,128)(2,1)S(1)}, u32[]{:S(2)}, u32[]{:S(2)}) collective-permute-start(bf16[64,512]{1,0:T(8,128)(2,1)S(1)} %get-tuple-element.38), channel_id=1, source_target_pairs={{0,10},{1,11},{2,8},{3,9},{4,14},{5,15},{6,12},{7,13},{8,2},{9,3},... | collective-permute-start | bytes 196616 | tf_op jit(solution)/shard_map/ppermute | solution.py:20
  7.5 14.6 %collective-permute-start = (bf16[2,64,512]{2,1,0:T(8,128)(2,1)S(1)}, bf16[2,64,512]{2,1,0:T(8,128)(2,1)S(1)}, u32[]{:S(2)}, u32[]{:S(2)}) collective-permute-start(bf16[2,64,512]{2,1,0:T(8,128)(2,1)S(1)} %get-tuple-element.26), channel_id=1, source_target_pairs={{0,2},{1,3},{2,0},{3,1},{4,6},{5,7},{6,4},{7,5},{8,10},{9,11},{10,... | collective-permute-start | bytes 393224 | tf_op jit(solution)/shard_map/ppermute | solution.py:20
  7.8 14.3 %collective-permute-start.1 = (bf16[2,64,512]{2,1,0:T(8,128)(2,1)S(1)}, bf16[2,64,512]{2,1,0:T(8,128)(2,1)S(1)}, u32[]{:S(2)}, u32[]{:S(2)}) collective-permute-start(bf16[2,64,512]{2,1,0:T(8,128)(2,1)S(1)} %get-tuple-element.27), channel_id=1, source_target_pairs={{0,4},{1,5},{2,6},{3,7},{4,0},{5,1},{6,2},{7,3},{8,12},{9,13},{10,... | collective-permute-start | bytes 393224 | tf_op jit(solution)/shard_map/ppermute | solution.py:20
  9.6 12.4 %collective-permute-start.2 = (bf16[2,64,512]{2,1,0:T(8,128)(2,1)S(1)}, bf16[2,64,512]{2,1,0:T(8,128)(2,1)S(1)}, u32[]{:S(2)}, u32[]{:S(2)}) collective-permute-start(bf16[2,64,512]{2,1,0:T(8,128)(2,1)S(1)} %get-tuple-element.28), channel_id=1, source_target_pairs={{0,6},{1,7},{2,4},{3,5},{4,2},{5,3},{6,0},{7,1},{8,14},{9,15},{10,... | collective-permute-start | bytes 393224 | tf_op jit(solution)/shard_map/ppermute | solution.py:20
  11.0 8.8 %collective-permute-start.12 = (bf16[64,512]{1,0:T(8,128)(2,1)S(1)}, bf16[64,512]{1,0:T(8,128)(2,1)S(1)}, u32[]{:S(2)}, u32[]{:S(2)}) collective-permute-start(bf16[64,512]{1,0:T(8,128)(2,1)S(1)} %get-tuple-element.39), channel_id=1, source_target_pairs={{0,12},{1,13},{2,14},{3,15},{4,8},{5,9},{6,10},{7,11},{8,4},{9,5},... | collective-permute-start | bytes 196616 | tf_op jit(solution)/shard_map/ppermute | solution.py:20
  15.1 7.0 %copy-start = (s32[16]{0:T(128)S(1)}, s32[16]{0:T(128)}, u32[]{:S(2)}) copy-start(s32[16]{0:T(128)} %spans.5) | copy-start | bytes 196
  15.1 7.0 %collective-permute-start.13 = (bf16[64,512]{1,0:T(8,128)(2,1)S(1)}, bf16[64,512]{1,0:T(8,128)(2,1)S(1)}, u32[]{:S(2)}, u32[]{:S(2)}) collective-permute-start(bf16[64,512]{1,0:T(8,128)(2,1)S(1)} %get-tuple-element.40), channel_id=1, source_target_pairs={{0,14},{1,15},{2,12},{3,13},{4,10},{5,11},{6,8},{7,9},{8,6},{9,7},... | collective-permute-start | bytes 196616 | tf_op jit(solution)/shard_map/ppermute | solution.py:20
  22.9 17.9 %collective-permute-start.14 = (bf16[2,64,512]{2,1,0:T(8,128)(2,1)S(1)}, bf16[2,64,512]{2,1,0:T(8,128)(2,1)S(1)}, u32[]{:S(2)}, u32[]{:S(2)}) collective-permute-start(bf16[2,64,512]{2,1,0:T(8,128)(2,1)S(1)} %get-tuple-element.42), channel_id=1, source_target_pairs={{0,2},{1,3},{2,0},{3,1},{4,6},{5,7},{6,4},{7,5},{8,10},{9,11},{10,... | collective-permute-start | bytes 393224 | tf_op jit(solution)/shard_map/ppermute | solution.py:20
  24.3 7.7 %collective-permute-start.3 = (bf16[64,512]{1,0:T(8,128)(2,1)S(1)}, bf16[64,512]{1,0:T(8,128)(2,1)S(1)}, u32[]{:S(2)}, u32[]{:S(2)}) collective-permute-start(bf16[64,512]{1,0:T(8,128)(2,1)S(1)} %get-tuple-element.29), channel_id=1, source_target_pairs={{0,8},{1,9},{2,10},{3,11},{4,12},{5,13},{6,14},{7,15},{8,0},{9,1},... | collective-permute-start | bytes 196616 | tf_op jit(solution)/shard_map/ppermute | solution.py:20
  24.8 11.1 %collective-permute-start.4 = (bf16[64,512]{1,0:T(8,128)(2,1)S(1)}, bf16[64,512]{1,0:T(8,128)(2,1)S(1)}, u32[]{:S(2)}, u32[]{:S(2)}) collective-permute-start(bf16[64,512]{1,0:T(8,128)(2,1)S(1)} %get-tuple-element.30), channel_id=1, source_target_pairs={{0,10},{1,11},{2,8},{3,9},{4,14},{5,15},{6,12},{7,13},{8,2},{9,3},... | collective-permute-start | bytes 196616 | tf_op jit(solution)/shard_map/ppermute | solution.py:20
  27.4 8.6 %collective-permute-start.5 = (bf16[64,512]{1,0:T(8,128)(2,1)S(1)}, bf16[64,512]{1,0:T(8,128)(2,1)S(1)}, u32[]{:S(2)}, u32[]{:S(2)}) collective-permute-start(bf16[64,512]{1,0:T(8,128)(2,1)S(1)} %get-tuple-element.31), channel_id=1, source_target_pairs={{0,12},{1,13},{2,14},{3,15},{4,8},{5,9},{6,10},{7,11},{8,4},{9,5},... | collective-permute-start | bytes 196616 | tf_op jit(solution)/shard_map/ppermute | solution.py:20
  30.5 7.2 %collective-permute-start.6 = (bf16[64,512]{1,0:T(8,128)(2,1)S(1)}, bf16[64,512]{1,0:T(8,128)(2,1)S(1)}, u32[]{:S(2)}, u32[]{:S(2)}) collective-permute-start(bf16[64,512]{1,0:T(8,128)(2,1)S(1)} %get-tuple-element.32), channel_id=1, source_target_pairs={{0,14},{1,15},{2,12},{3,13},{4,10},{5,11},{6,8},{7,9},{8,6},{9,7},... | collective-permute-start | bytes 196616 | tf_op jit(solution)/shard_map/ppermute | solution.py:20
  31.9 10.2 %collective-permute-start.15 = (bf16[2,64,512]{2,1,0:T(8,128)(2,1)S(1)}, bf16[2,64,512]{2,1,0:T(8,128)(2,1)S(1)}, u32[]{:S(2)}, u32[]{:S(2)}) collective-permute-start(bf16[2,64,512]{2,1,0:T(8,128)(2,1)S(1)} %get-tuple-element.43), channel_id=1, source_target_pairs={{0,4},{1,5},{2,6},{3,7},{4,0},{5,1},{6,2},{7,3},{8,12},{9,13},{10,... | collective-permute-start | bytes 393224 | tf_op jit(solution)/shard_map/ppermute | solution.py:20
  35.9 6.7 %collective-permute-start.16 = (bf16[2,64,512]{2,1,0:T(8,128)(2,1)S(1)}, bf16[2,64,512]{2,1,0:T(8,128)(2,1)S(1)}, u32[]{:S(2)}, u32[]{:S(2)}) collective-permute-start(bf16[2,64,512]{2,1,0:T(8,128)(2,1)S(1)} %get-tuple-element.44), channel_id=1, source_target_pairs={{0,6},{1,7},{2,4},{3,5},{4,2},{5,3},{6,0},{7,1},{8,14},{9,15},{10,... | collective-permute-start | bytes 393224 | tf_op jit(solution)/shard_map/ppermute | solution.py:20
  38.6 6.4 %collective-permute-start.7 = (bf16[2,64,512]{2,1,0:T(8,128)(2,1)S(1)}, bf16[2,64,512]{2,1,0:T(8,128)(2,1)S(1)}, u32[]{:S(2)}, u32[]{:S(2)}) collective-permute-start(bf16[2,64,512]{2,1,0:T(8,128)(2,1)S(1)} %get-tuple-element.34), channel_id=1, source_target_pairs={{0,2},{1,3},{2,0},{3,1},{4,6},{5,7},{6,4},{7,5},{8,10},{9,11},{10,... | collective-permute-start | bytes 393224 | tf_op jit(solution)/shard_map/ppermute | solution.py:20
  39.0 6.2 %collective-permute-start.8 = (bf16[2,64,512]{2,1,0:T(8,128)(2,1)S(1)}, bf16[2,64,512]{2,1,0:T(8,128)(2,1)S(1)}, u32[]{:S(2)}, u32[]{:S(2)}) collective-permute-start(bf16[2,64,512]{2,1,0:T(8,128)(2,1)S(1)} %get-tuple-element.35), channel_id=1, source_target_pairs={{0,4},{1,5},{2,6},{3,7},{4,0},{5,1},{6,2},{7,3},{8,12},{9,13},{10,... | collective-permute-start | bytes 393224 | tf_op jit(solution)/shard_map/ppermute | solution.py:20
  40.8 6.6 %collective-permute-start.9 = (bf16[2,64,512]{2,1,0:T(8,128)(2,1)S(1)}, bf16[2,64,512]{2,1,0:T(8,128)(2,1)S(1)}, u32[]{:S(2)}, u32[]{:S(2)}) collective-permute-start(bf16[2,64,512]{2,1,0:T(8,128)(2,1)S(1)} %get-tuple-element.36), channel_id=1, source_target_pairs={{0,6},{1,7},{2,4},{3,5},{4,2},{5,3},{6,0},{7,1},{8,14},{9,15},{10,... | collective-permute-start | bytes 393224 | tf_op jit(solution)/shard_map/ppermute | solution.py:20
  42.7 4.8 %collective-permute-start.18 = (bf16[4,64,512]{2,1,0:T(8,128)(2,1)S(1)}, bf16[4,64,512]{2,1,0:T(8,128)(2,1)S(1)}, u32[]{:S(2)}, u32[]{:S(2)}) collective-permute-start(bf16[4,64,512]{2,1,0:T(8,128)(2,1)S(1)} %hand_over.3), channel_id=1, source_target_pairs={{0,1},{1,0},{2,3},{3,2},{4,5},{5,4},{6,7},{7,6},{8,9},{9,8},{10,11... | collective-permute-start | bytes 786440 | tf_op jit(solution)/shard_map/ppermute | solution.py:20
  47.4 1.6 %copy-start.1 = (s32[32]{0:T(128)S(1)}, s32[32]{0:T(128)}, u32[]{:S(2)}) copy-start(s32[32]{0:T(128)} %table.1) | copy-start | bytes 388
  47.4 1.6 %collective-permute-start.17 = (bf16[4,64,512]{2,1,0:T(8,128)(2,1)S(1)}, bf16[4,64,512]{2,1,0:T(8,128)(2,1)S(1)}, u32[]{:S(2)}, u32[]{:S(2)}) collective-permute-start(bf16[4,64,512]{2,1,0:T(8,128)(2,1)S(1)} %hand_over.2), channel_id=1, source_target_pairs={{0,1},{1,0},{2,3},{3,2},{4,5},{5,4},{6,7},{7,6},{8,9},{9,8},{10,11... | collective-permute-start | bytes 786440 | tf_op jit(solution)/shard_map/ppermute | solution.py:20
where the time goes:
time: 50.8 us; the launch traced here: 50.7 us
  starting transfers between devices  27.9 us (55%)
  waiting for transfers between devices  17.2 us (34%)
  Pallas kernels  5.49 us (11%)
    ppermute x19, starting transfers between devices, swap(): return lax.ppermute(x, AXES, [(i, i ^ distance) for i in range(size)])  27.9 us
    ppermute x19, waiting for transfers between devices, swap(): return lax.ppermute(x, AXES, [(i, i ^ distance) for i in range(size)])  17.2 us
    pallas_call x1, Pallas kernels, by_permutes(): pl.pallas_call(functools.partial(prepare, chips, piece), out_shape=[one]...  2.08 us
    pallas_call x2, Pallas kernels, by_permutes(): pl.pallas_call(functools.partial(route, chips, kind), out_shape=[two] * n...  1.72 us
    pallas_call x1, Pallas kernels, by_permutes(): pl.pallas_call(functools.partial(finish, near, piece), out_shape=jax.Shap...  1.65 us
  transfers between devices with their start and end apart: 19, of which 9 were waited for; matrix products, arithmetic and copies ran while one was open for 0% of the time, Pallas kernels for 2%

commit v1 on v0

v1 whole, which is shorter than its diff:
```python
import functools

import jax
import jax.numpy as jnp
from jax import lax
from jax.experimental import pallas as pl
from jax.experimental.pallas import tpu as pltpu
from jax.sharding import PartitionSpec as P

PAGE = 128
SUBLANES = 16
MIN_BYTES = 1 << 16
AXES = ("ctx", "head")
VMEM = pl.BlockSpec(memory_space=pltpu.VMEM)
SMEM = pl.BlockSpec(memory_space=pltpu.SMEM)
SMALL = pltpu.CompilerParams(vmem_limit_bytes=8 << 20)
HBM = pl.BlockSpec(memory_space=pltpu.HBM)


def swap(x, size, distances):
    pairs = [(i, 2 * (i // 2 ^ distances[i % 2]) + i % 2) for i in range(size)]
    return lax.ppermute(x, AXES, pairs)


def trade(x, size):
    return lax.ppermute(x, AXES, [(i, i ^ 1) for i in range(size)])


def prepare(chips, piece, spans, data, *refs):
    outs, table, table_sem, sems = refs[:-3], *refs[-3:]
    near, lanes = chips // 2, chips // 4
    me = lax.axis_index("ctx")
    load = pltpu.make_async_copy(spans, table, table_sem)
    load.start()
    load.wait()
    first_low = table[2 * me] < chips
    stay = jnp.where((me < near) == first_low, 0, 1)
    copies = []

    def rows(block, i):
        return pl.ds(pl.multiple_of((block * lanes + i) * piece, piece), piece)

    for kind in range(2):
        for i in range(lanes):
            copies.append((data.at[kind, rows(1 - stay, i), :], outs[len(copies)]))
    for i in range(lanes):
        copies.append((data.at[:, rows(stay, i), :], outs[len(copies)]))
    copies = [pltpu.make_async_copy(*c, sems.at[n]) for n, c in enumerate(copies)]
    for copy in copies:
        copy.start()
    for copy in copies:
        copy.wait()


def route(chips, kind, spans, *refs):
    near, lanes = chips // 2, chips // 4
    ins, outs = refs[:chips], refs[chips:]
    me, head = lax.axis_index("ctx"), lax.axis_index("head")
    local, low = lax.rem(me, near), me < near
    for n in range(chips):
        group, i = n // lanes, n % lanes
        core = head if group % 2 == 0 else 1 - head
        source = me ^ ((group // 2) * near + i + core * lanes)
        a, b = spans[2 * source], spans[2 * source + 1]
        span = jnp.where((a < chips) == low, a, b)
        distance = lax.rem(span // 2, near) ^ local
        for j in range(near):

            @pl.when((distance == j) & (lax.rem(span, 2) == head))
            def _(n=n, j=j, group=group):
                outs[j][...] = ins[n][kind] if group < 2 else ins[n][...]


def finish(chips, piece, spans, table, *refs):
    near, lanes = chips // 2, chips // 4
    ins, (out, sems) = refs[: 2 * near], refs[2 * near :]
    pages, width = out.shape[1], out.shape[3] // 2
    me = lax.axis_index("ctx")
    device = 2 * me + lax.axis_index("head")
    source = jnp.int32(0)
    for c in range(chips):
        here = (spans[2 * c] == device) | (spans[2 * c + 1] == device)
        source = jnp.where(here, c, source)
    strip = min(piece, PAGE)
    copies = []
    for n, ref in enumerate(ins):
        kind, j = n // near, n % near
        part = lax.rem(me ^ j ^ source, near)
        cols = pl.ds(pl.multiple_of(part // lanes * width, width), width)
        for k in range(piece // strip):
            row = lax.rem(part, lanes) * piece + k * strip
            slot = table[device * pages + row // PAGE] - device * pages
            rows = pl.ds(pl.multiple_of(lax.rem(row, PAGE), strip), strip)
            src = ref.at[pl.ds(k * strip, strip), :]
            dst = out.at[kind, slot, rows, cols]
            copies.append(pltpu.make_async_copy(src, dst, sems.at[len(copies)]))
    for copy in copies:
        copy.start()
    for copy in copies:
        copy.wait()


def piece_rows(chips, span_len):
    return span_len // max(chips // 4, 1)


def by_permutes(keys_values, span_order, page_table):
    chips = lax.axis_size("ctx")
    size, near, lanes = 2 * chips, chips // 2, chips // 4
    width = keys_values.shape[2]
    span_len = keys_values.shape[1] // 2
    piece = piece_rows(chips, span_len)
    dtype = keys_values.dtype
    one = jax.ShapeDtypeStruct((piece, width), dtype)
    two = jax.ShapeDtypeStruct((2, piece, width), dtype)
    n = 3 * lanes
    pieces = pl.pallas_call(
        functools.partial(prepare, chips, piece),
        out_shape=[one] * (2 * lanes) + [two] * lanes,
        in_specs=[HBM, HBM],
        out_specs=[VMEM] * n,
        scratch_shapes=[
            pltpu.SMEM(span_order.shape, span_order.dtype),
            pltpu.SemaphoreType.DMA,
            pltpu.SemaphoreType.DMA((n,)),
        ],
        name="prepare",
        compiler_params=SMALL,
    )(
        pltpu.with_memory_space_constraint(span_order, pltpu.HBM),
        pltpu.with_memory_space_constraint(keys_values, pltpu.HBM),
    )
    far = [
        [swap(pieces[kind * lanes + i], size, (near + i, near + i + lanes)) for i in range(lanes)]
        for kind in range(2)
    ]
    stay = [swap(pieces[2 * lanes + i], size, (i, i + lanes)) for i in range(lanes)]
    far_other = [[trade(far[kind][i], size) for i in range(lanes)] for kind in range(2)]
    stay_other = [trade(stay[i], size) for i in range(lanes)]
    held = []
    for kind in range(2):
        routed = pl.pallas_call(
            functools.partial(route, chips, kind),
            out_shape=[one] * near,
            in_specs=[SMEM] + [VMEM] * chips,
            out_specs=[VMEM] * near,
            name="route",
            compiler_params=SMALL,
        )(span_order, *stay, *stay_other, *far[kind], *far_other[kind])
        held += [routed[0]] + [swap(routed[j], size, (j, j)) for j in range(1, near)]
    return pl.pallas_call(
        functools.partial(finish, chips, piece),
        out_shape=jax.ShapeDtypeStruct((2, span_len // PAGE, PAGE, 2 * width), dtype),
        in_specs=[SMEM, SMEM] + [VMEM] * (2 * near),
        out_specs=HBM,
        scratch_shapes=[pltpu.SemaphoreType.DMA((2 * near * max(piece // PAGE, 1),))],
        name="finish",
        compiler_params=SMALL,
    )(span_order, page_table, *held)


def by_all_to_alls(keys_values, span_order, page_table):
    tok_rows = keys_values.shape[1]
    width = keys_values.shape[2]
    span_len = tok_rows // 2
    per_span = span_len // PAGE
    ctx_index = lax.axis_index("ctx")
    spans = lax.axis_size("ctx") * lax.axis_size("head")
    half = spans // 2
    piece = span_len // half

    first_span = lax.dynamic_index_in_dim(span_order, 2 * ctx_index, keepdims=False)
    flip = first_span >= half
    blocks = keys_values.reshape(2, 2, half, piece, width)
    low = jnp.where(flip, blocks[:, 1], blocks[:, 0])
    high = jnp.where(flip, blocks[:, 0], blocks[:, 1])
    spread = jnp.stack([low, high], axis=0).transpose(0, 2, 1, 3, 4)
    spread = spread.reshape(spans, 2, piece, width)
    spread = lax.all_to_all(spread, AXES, split_axis=0, concat_axis=0, tiled=True)

    device = 2 * ctx_index + lax.axis_index("head")
    base = (device // half) * half
    wanted = base + jnp.arange(half, dtype=jnp.int32)
    chips = jnp.arange(spans, dtype=jnp.int32) // 2
    holder = jnp.sum(jnp.where(span_order[None, :] == wanted[:, None], chips[None, :], 0), axis=1)
    spread = spread.reshape(half, 2, 2, piece, width)
    routed = jnp.take(spread, holder, axis=0, mode="clip")
    groups = [list(range(half)), list(range(half, spans))]
    routed = lax.all_to_all(
        routed, AXES, split_axis=0, concat_axis=0, tiled=True, axis_index_groups=groups
    )
    rows = routed.transpose(2, 0, 3, 1, 4).reshape(2, per_span, PAGE, 2 * width)
    slots = lax.dynamic_slice_in_dim(page_table, device * per_span, per_span) - device * per_span
    order = jnp.sum(
        jnp.where(
            slots[None, :] == jnp.arange(per_span, dtype=jnp.int32)[:, None],
            jnp.arange(per_span, dtype=jnp.int32)[None, :],
            0,
        ),
        axis=1,
    )
    return jnp.take(rows, order, axis=1, mode="clip")


def pipelined(chips, rows, width, itemsize):
    piece = piece_rows(chips, rows // 2)
    whole = chips >= 4 and chips & (chips - 1) == 0 and piece % SUBLANES == 0
    return whole and piece * width * itemsize >= MIN_BYTES


def per_device(keys_values, span_order, page_table):
    _, rows, width = keys_values.shape
    if pipelined(lax.axis_size("ctx"), rows, width, keys_values.dtype.itemsize):
        return by_permutes(keys_values, span_order, page_table)
    return by_all_to_alls(keys_values, span_order, page_table)


def solution(mesh):
    in_specs = (P(None, ("groups", "ctx"), "head"), P("groups"), P("groups"))
    out_specs = P(None, ("groups", "ctx", "head"), None, None)
    return jax.shard_map(
        per_device, mesh=mesh, in_specs=in_specs, out_specs=out_specs, check_vma=False
    )
```

time: 50.8 us -> 51.1 us (level)
  waiting for transfers between devices: 17.2 us -> 16 us
  starting transfers between devices: 27.9 us -> 28.8 us
  local copies, waits for them, and re-layouts: 0.01 us -> 0.66 us
    ppermute x19 -> x18, waiting for transfers between devices: 17.2 us -> 16 us  [the longest x12 16 us: swap(): return lax.ppermute(x, AXES, pairs)]
    ppermute x19 -> x18, starting transfers between devices: 27.9 us -> 28.8 us  [the longest x12 20.7 us: swap(): return lax.ppermute(x, AXES, pairs)]
    unnamed x4, local copies, waits for them, and re-layouts: 0.01 us -> 0.66 us
    pallas_call x5 -> x3, Pallas kernels: 3.41 us -> 3.36 us  [the longest x2 1.75 us: by_permutes(): pl.pallas_call(functools.partial(route, chips, kind), out_shape=[one] * n...]
  transfers between devices with their start and end apart: 19 -> 18, of which waited for: 9 -> 5; matrix products, arithmetic and copies ran while one was open for 0% -> 0% of each run, Pallas kernels for 2% -> 3%
where the time goes in v1:
time: 51.1 us; the launch traced here: 50.9 us
  starting transfers between devices  28.8 us (56%)
  waiting for transfers between devices  16 us (31%)
  Pallas kernels  5.38 us (11%)
  local copies, waits for them, and re-layouts  0.66 us (1%)
    ppermute x12, starting transfers between devices, swap(): return lax.ppermute(x, AXES, pairs)  20.7 us
    ppermute x12, waiting for transfers between devices, swap(): return lax.ppermute(x, AXES, pairs)  16 us
    ppermute x6, starting transfers between devices, trade(): return lax.ppermute(x, AXES, [(i, i ^ 1) for i in range(size)])  8.07 us
    pallas_call x1, Pallas kernels, by_permutes(): pl.pallas_call(functools.partial(prepare, chips, piece), out_shape=[one]...  2.02 us
    pallas_call x2, Pallas kernels, by_permutes(): pl.pallas_call(functools.partial(route, chips, kind), out_shape=[one] * n...  1.75 us
    pallas_call x1, Pallas kernels, by_permutes(): pl.pallas_call(functools.partial(finish, chips, piece), out_shape=jax.Sha...  1.61 us
  transfers between devices with their start and end apart: 18, of which 5 were waited for; matrix products, arithmetic and copies ran while one was open for 0% of the time, Pallas kernels for 3%

profile of v1, /device:TPU:0, one launch (start us, length us, event | category | flops | bytes accessed | tf_op | source)
XLA Modules:
  0.0 50.9 jit_solution(17501324185389650862)
XLA Ops:
  0.0 2.0 %prepare.1 = (bf16[128,512]{1,0:T(8,128)(2,1)S(1)}, bf16[128,512]{1,0:T(8,128)(2,1)S(1)}, bf16[128,512]{1,0:T(8,128)(2,1)S(1)}, bf16[128,512]{1,0:T(8,128)(2,1)S...) custom-call(s32[16]{0:T(128)} %spans.7, bf16[2,512,512]{2,1,0:T(8,128)(2,1)} %data.1), custom_call_target="tpu_custom_call" | custom-call | tf_op jit(solution)/shard_map/prepare/pallas_call | solution.py:117
  2.0 0.7 %collective-permute-start = (bf16[2,128,512]{2,1,0:T(8,128)(2,1)S(1)}, bf16[2,128,512]{2,1,0:T(8,128)(2,1)S(1)}, u32[]{:S(2)}, u32[]{:S(2)}) collective-permute-start(bf16[2,128,512]{2,1,0:T(8,128)(2,1)S(1)} %get-tuple-element.19), channel_id=1, source_target_pairs={{0,0},{1,5},{2,2},{3,7},{4,4},{5,1},{6,6},{7,3},{8,8},{9,13},{10,1... | collective-permute-start | bytes 786440 | tf_op jit(solution)/shard_map/ppermute | solution.py:22
  2.7 3.0 %collective-permute-start.1 = (bf16[2,128,512]{2,1,0:T(8,128)(2,1)S(1)}, bf16[2,128,512]{2,1,0:T(8,128)(2,1)S(1)}, u32[]{:S(2)}, u32[]{:S(2)}) collective-permute-start(bf16[2,128,512]{2,1,0:T(8,128)(2,1)S(1)} %get-tuple-element.20), channel_id=1, source_target_pairs={{0,2},{1,7},{2,0},{3,5},{4,6},{5,3},{6,4},{7,1},{8,10},{9,15},{10,... | collective-permute-start | bytes 786440 | tf_op jit(solution)/shard_map/ppermute | solution.py:22
  5.7 2.6 %collective-permute-start.11 = (bf16[128,512]{1,0:T(8,128)(2,1)S(1)}, bf16[128,512]{1,0:T(8,128)(2,1)S(1)}, u32[]{:S(2)}, u32[]{:S(2)}) collective-permute-start(bf16[128,512]{1,0:T(8,128)(2,1)S(1)} %get-tuple-element.27), channel_id=1, source_target_pairs={{0,8},{1,13},{2,10},{3,15},{4,12},{5,9},{6,14},{7,11},{8,0},{9,5},... | collective-permute-start | bytes 393224 | tf_op jit(solution)/shard_map/ppermute | solution.py:22
  8.3 0.0 collective-permute-start.12
  8.3 0.0 copy-start
  8.3 2.9 %collective-permute-start.4 = (bf16[128,512]{1,0:T(8,128)(2,1)S(1)}, bf16[128,512]{1,0:T(8,128)(2,1)S(1)}, u32[]{:S(2)}, u32[]{:S(2)}) collective-permute-start(bf16[128,512]{1,0:T(8,128)(2,1)S(1)} %get-tuple-element.21), channel_id=1, source_target_pairs={{0,8},{1,13},{2,10},{3,15},{4,12},{5,9},{6,14},{7,11},{8,0},{9,5},... | collective-permute-start | bytes 393224 | tf_op jit(solution)/shard_map/ppermute | solution.py:22
  11.2 0.0 collective-permute-done.refs_0_
  11.2 3.0 %collective-permute-start.2 = (bf16[2,128,512]{2,1,0:T(8,128)(2,1)S(1)}, bf16[2,128,512]{2,1,0:T(8,128)(2,1)S(1)}, u32[]{:S(2)}, u32[]{:S(2)}) collective-permute-start(bf16[2,128,512]{2,1,0:T(8,128)(2,1)S(1)} %collective-permute-done.refs_0_), channel_id=1, source_target_pairs={{0,1},{1,0},{2,3},{3,2},{4,5},{5,4},{6,7},{7,6},{8,9},{9,8},{10,11... | collective-permute-start | bytes 786440 | tf_op jit(solution)/shard_map/ppermute | solution.py:26
  14.3 0.0 collective-permute-done.1.refs_1_
  14.3 2.5 %collective-permute-start.3 = (bf16[2,128,512]{2,1,0:T(8,128)(2,1)S(1)}, bf16[2,128,512]{2,1,0:T(8,128)(2,1)S(1)}, u32[]{:S(2)}, u32[]{:S(2)}) collective-permute-start(bf16[2,128,512]{2,1,0:T(8,128)(2,1)S(1)} %collective-permute-done.1.refs_1_), channel_id=1, source_target_pairs={{0,1},{1,0},{2,3},{3,2},{4,5},{5,4},{6,7},{7,6},{8,9},{9,8},{10,11... | collective-permute-start | bytes 786440 | tf_op jit(solution)/shard_map/ppermute | solution.py:26
  16.8 0.0 collective-permute-done.11.refs_4_
  16.8 4.4 %collective-permute-start.5 = (bf16[128,512]{1,0:T(8,128)(2,1)S(1)}, bf16[128,512]{1,0:T(8,128)(2,1)S(1)}, u32[]{:S(2)}, u32[]{:S(2)}) collective-permute-start(bf16[128,512]{1,0:T(8,128)(2,1)S(1)} %get-tuple-element.22), channel_id=1, source_target_pairs={{0,10},{1,15},{2,8},{3,13},{4,14},{5,11},{6,12},{7,9},{8,2},{9,7},... | collective-permute-start | bytes 393224 | tf_op jit(solution)/shard_map/ppermute | solution.py:22
  21.3 0.0 collective-permute-done.12.refs_5_
  21.3 2.0 %collective-permute-start.13 = (bf16[128,512]{1,0:T(8,128)(2,1)S(1)}, bf16[128,512]{1,0:T(8,128)(2,1)S(1)}, u32[]{:S(2)}, u32[]{:S(2)}) collective-permute-start(bf16[128,512]{1,0:T(8,128)(2,1)S(1)} %collective-permute-done.11.refs_4_), channel_id=1, source_target_pairs={{0,1},{1,0},{2,3},{3,2},{4,5},{5,4},{6,7},{7,6},{8,9},{9,8},{10,11... | collective-permute-start | bytes 393224 | tf_op jit(solution)/shard_map/ppermute | solution.py:26
  23.2 5.6 %collective-permute-done.4.refs_4_ = bf16[128,512]{1,0:T(8,128)(2,1)S(1)} collective-permute-done((bf16[128,512]{1,0:T(8,128)(2,1)S(1)}, bf16[128,512]{1,0:T(8,128)(2,1)S(1)}, u32[]{:S(2)}, u32[]{:S(2)}) %collective-permute-start.4) | collective-permute-done | bytes 131104 | tf_op jit(solution)/shard_map/ppermute | solution.py:22
  28.9 0.0 collective-permute-start.14
  28.9 3.2 %collective-permute-done.5.refs_5_ = bf16[128,512]{1,0:T(8,128)(2,1)S(1)} collective-permute-done((bf16[128,512]{1,0:T(8,128)(2,1)S(1)}, bf16[128,512]{1,0:T(8,128)(2,1)S(1)}, u32[]{:S(2)}, u32[]{:S(2)}) %collective-permute-start.5) | collective-permute-done | bytes 131104 | tf_op jit(solution)/shard_map/ppermute | solution.py:22
  32.1 0.0 collective-permute-start.6
  32.1 0.0 collective-permute-done.13.refs_6_
  32.1 0.5 collective-permute-start.7
  32.6 0.0 collective-permute-done.14.refs_7_
  32.6 0.0 collective-permute-done.2.refs_2_
  32.6 0.0 collective-permute-done.3.refs_3_
  32.6 0.0 copy-done
  32.6 0.9 %route.3 = (bf16[128,512]{1,0:T(8,128)(2,1)S(1)}, bf16[128,512]{1,0:T(8,128)(2,1)S(1)}, bf16[128,512]{1,0:T(8,128)(2,1)S(1)}, bf16[128,512]{1,0:T(8,128)(2,1)S(1)}) custom-call(s32[16]{0:T(128)S(1)} %copy-done, bf16[2,128,512]{2,1,0:T(8,128)(2,1)S(1)} %collective-permute-done.refs_0_, bf16[2,128,512]{2,1,0:T(8,128)(2,1)S(1)} %collective-permute-done.1.refs_1_, ...), custom_call_target="tpu_custom_call" | custom-call | tf_op jit(solution)/shard_map/route/pallas_call | solution.py:142
  33.5 1.1 %collective-permute-start.15 = (bf16[128,512]{1,0:T(8,128)(2,1)S(1)}, bf16[128,512]{1,0:T(8,128)(2,1)S(1)}, u32[]{:S(2)}, u32[]{:S(2)}) collective-permute-start(bf16[128,512]{1,0:T(8,128)(2,1)S(1)} %get-tuple-element.30), channel_id=1, source_target_pairs={{0,2},{1,3},{2,0},{3,1},{4,6},{5,7},{6,4},{7,5},{8,10},{9,11},{10,... | collective-permute-start | bytes 393224 | tf_op jit(solution)/shard_map/ppermute | solution.py:22
  34.7 0.9 %collective-permute-start.16 = (bf16[128,512]{1,0:T(8,128)(2,1)S(1)}, bf16[128,512]{1,0:T(8,128)(2,1)S(1)}, u32[]{:S(2)}, u32[]{:S(2)}) collective-permute-start(bf16[128,512]{1,0:T(8,128)(2,1)S(1)} %get-tuple-element.31), channel_id=1, source_target_pairs={{0,4},{1,5},{2,6},{3,7},{4,0},{5,1},{6,2},{7,3},{8,12},{9,13},{10,... | collective-permute-start | bytes 393224 | tf_op jit(solution)/shard_map/ppermute | solution.py:22
  35.6 1.5 %collective-permute-start.17 = (bf16[128,512]{1,0:T(8,128)(2,1)S(1)}, bf16[128,512]{1,0:T(8,128)(2,1)S(1)}, u32[]{:S(2)}, u32[]{:S(2)}) collective-permute-start(bf16[128,512]{1,0:T(8,128)(2,1)S(1)} %get-tuple-element.32), channel_id=1, source_target_pairs={{0,6},{1,7},{2,4},{3,5},{4,2},{5,3},{6,0},{7,1},{8,14},{9,15},{10,... | collective-permute-start | bytes 393224 | tf_op jit(solution)/shard_map/ppermute | solution.py:22
  37.1 0.0 collective-permute-done.6.refs_6_
  37.1 0.0 collective-permute-done.7.refs_7_
  37.1 0.9 %route.2 = (bf16[128,512]{1,0:T(8,128)(2,1)S(1)}, bf16[128,512]{1,0:T(8,128)(2,1)S(1)}, bf16[128,512]{1,0:T(8,128)(2,1)S(1)}, bf16[128,512]{1,0:T(8,128)(2,1)S(1)}) custom-call(s32[16]{0:T(128)S(1)} %copy-done, bf16[2,128,512]{2,1,0:T(8,128)(2,1)S(1)} %collective-permute-done.refs_0_, bf16[2,128,512]{2,1,0:T(8,128)(2,1)S(1)} %collective-permute-done.1.refs_1_, ...), custom_call_target="tpu_custom_call" | custom-call | tf_op jit(solution)/shard_map/route/pallas_call | solution.py:142
  38.0 1.5 %collective-permute-start.10 = (bf16[128,512]{1,0:T(8,128)(2,1)S(1)}, bf16[128,512]{1,0:T(8,128)(2,1)S(1)}, u32[]{:S(2)}, u32[]{:S(2)}) collective-permute-start(bf16[128,512]{1,0:T(8,128)(2,1)S(1)} %get-tuple-element.26), channel_id=1, source_target_pairs={{0,6},{1,7},{2,4},{3,5},{4,2},{5,3},{6,0},{7,1},{8,14},{9,15},{10,... | collective-permute-start | bytes 393224 | tf_op jit(solution)/shard_map/ppermute | solution.py:22
  39.4 1.4 %collective-permute-start.8 = (bf16[128,512]{1,0:T(8,128)(2,1)S(1)}, bf16[128,512]{1,0:T(8,128)(2,1)S(1)}, u32[]{:S(2)}, u32[]{:S(2)}) collective-permute-start(bf16[128,512]{1,0:T(8,128)(2,1)S(1)} %get-tuple-element.24), channel_id=1, source_target_pairs={{0,2},{1,3},{2,0},{3,1},{4,6},{5,7},{6,4},{7,5},{8,10},{9,11},{10,... | collective-permute-start | bytes 393224 | tf_op jit(solution)/shard_map/ppermute | solution.py:22
  40.8 0.0 collective-permute-done.15.refs_5_
  40.8 0.7 %collective-permute-start.9 = (bf16[128,512]{1,0:T(8,128)(2,1)S(1)}, bf16[128,512]{1,0:T(8,128)(2,1)S(1)}, u32[]{:S(2)}, u32[]{:S(2)}) collective-permute-start(bf16[128,512]{1,0:T(8,128)(2,1)S(1)} %get-tuple-element.25), channel_id=1, source_target_pairs={{0,4},{1,5},{2,6},{3,7},{4,0},{5,1},{6,2},{7,3},{8,12},{9,13},{10,... | collective-permute-start | bytes 393224 | tf_op jit(solution)/shard_map/ppermute | solution.py:22
  41.5 0.0 collective-permute-done.16.refs_6_
  41.5 2.8 %collective-permute-done.17.refs_7_ = bf16[128,512]{1,0:T(8,128)(2,1)S(1)} collective-permute-done((bf16[128,512]{1,0:T(8,128)(2,1)S(1)}, bf16[128,512]{1,0:T(8,128)(2,1)S(1)}, u32[]{:S(2)}, u32[]{:S(2)}) %collective-permute-start.17) | collective-permute-done | bytes 131104 | tf_op jit(solution)/shard_map/ppermute | solution.py:22
  44.3 2.8 %collective-permute-done.10.refs_3_ = bf16[128,512]{1,0:T(8,128)(2,1)S(1)} collective-permute-done((bf16[128,512]{1,0:T(8,128)(2,1)S(1)}, bf16[128,512]{1,0:T(8,128)(2,1)S(1)}, u32[]{:S(2)}, u32[]{:S(2)}) %collective-permute-start.10) | collective-permute-done | bytes 131104 | tf_op jit(solution)/shard_map/ppermute | solution.py:22
  47.1 1.6 %collective-permute-done.8.refs_1_ = bf16[128,512]{1,0:T(8,128)(2,1)S(1)} collective-permute-done((bf16[128,512]{1,0:T(8,128)(2,1)S(1)}, bf16[128,512]{1,0:T(8,128)(2,1)S(1)}, u32[]{:S(2)}, u32[]{:S(2)}) %collective-permute-start.8) | collective-permute-done | bytes 131104 | tf_op jit(solution)/shard_map/ppermute | solution.py:22
  48.6 0.0 collective-permute-done.9.refs_2_
  48.6 0.0 copy-start.1
  48.6 0.7 %copy-done.1 = s32[32]{0:T(128)S(1)} copy-done((s32[32]{0:T(128)S(1)}, s32[32]{0:T(128)}, u32[]{:S(2)}) %copy-start.1) | copy-done | bytes 152
  49.3 1.6 %finish.1 = bf16[2,2,128,1024]{3,2,1,0:T(8,128)(2,1)} custom-call(s32[16]{0:T(128)S(1)} %copy-done, s32[32]{0:T(128)S(1)} %copy-done.1, bf16[128,512]{1,0:T(8,128)(2,1)S(1)} %get-tuple-element.23.refs_0_, bf16[128,512]{1,0:T(8,128)(2,1)S(1)} %collective-permute-done.8.refs_1_, bf16[128,512]{1,0:T(8,128)(2,1)S(1)} %collective-permute-done.9.refs_2_, ...), custom_call_target="tpu_custom_call" | custom-call | tf_op jit(solution)/shard_map/finish/pallas_call | solution.py:151
Async XLA Ops:
  2.0 9.2 %collective-permute-start = (bf16[2,128,512]{2,1,0:T(8,128)(2,1)S(1)}, bf16[2,128,512]{2,1,0:T(8,128)(2,1)S(1)}, u32[]{:S(2)}, u32[]{:S(2)}) collective-permute-start(bf16[2,128,512]{2,1,0:T(8,128)(2,1)S(1)} %get-tuple-element.19), channel_id=1, source_target_pairs={{0,0},{1,5},{2,2},{3,7},{4,4},{5,1},{6,6},{7,3},{8,8},{9,13},{10,1... | collective-permute-start | bytes 786440 | tf_op jit(solution)/shard_map/ppermute | solution.py:22
  2.7 11.6 %collective-permute-start.1 = (bf16[2,128,512]{2,1,0:T(8,128)(2,1)S(1)}, bf16[2,128,512]{2,1,0:T(8,128)(2,1)S(1)}, u32[]{:S(2)}, u32[]{:S(2)}) collective-permute-start(bf16[2,128,512]{2,1,0:T(8,128)(2,1)S(1)} %get-tuple-element.20), channel_id=1, source_target_pairs={{0,2},{1,7},{2,0},{3,5},{4,6},{5,3},{6,4},{7,1},{8,10},{9,15},{10,... | collective-permute-start | bytes 786440 | tf_op jit(solution)/shard_map/ppermute | solution.py:22
  5.7 11.1 %collective-permute-start.11 = (bf16[128,512]{1,0:T(8,128)(2,1)S(1)}, bf16[128,512]{1,0:T(8,128)(2,1)S(1)}, u32[]{:S(2)}, u32[]{:S(2)}) collective-permute-start(bf16[128,512]{1,0:T(8,128)(2,1)S(1)} %get-tuple-element.27), channel_id=1, source_target_pairs={{0,8},{1,13},{2,10},{3,15},{4,12},{5,9},{6,14},{7,11},{8,0},{9,5},... | collective-permute-start | bytes 393224 | tf_op jit(solution)/shard_map/ppermute | solution.py:22
  8.3 12.9 %collective-permute-start.12 = (bf16[128,512]{1,0:T(8,128)(2,1)S(1)}, bf16[128,512]{1,0:T(8,128)(2,1)S(1)}, u32[]{:S(2)}, u32[]{:S(2)}) collective-permute-start(bf16[128,512]{1,0:T(8,128)(2,1)S(1)} %get-tuple-element.28), channel_id=1, source_target_pairs={{0,10},{1,15},{2,8},{3,13},{4,14},{5,11},{6,12},{7,9},{8,2},{9,7},... | collective-permute-start | bytes 393224 | tf_op jit(solution)/shard_map/ppermute | solution.py:22
  8.3 24.3 %copy-start = (s32[16]{0:T(128)S(1)}, s32[16]{0:T(128)}, u32[]{:S(2)}) copy-start(s32[16]{0:T(128)} %spans.7) | copy-start | bytes 196
  8.3 20.6 %collective-permute-start.4 = (bf16[128,512]{1,0:T(8,128)(2,1)S(1)}, bf16[128,512]{1,0:T(8,128)(2,1)S(1)}, u32[]{:S(2)}, u32[]{:S(2)}) collective-permute-start(bf16[128,512]{1,0:T(8,128)(2,1)S(1)} %get-tuple-element.21), channel_id=1, source_target_pairs={{0,8},{1,13},{2,10},{3,15},{4,12},{5,9},{6,14},{7,11},{8,0},{9,5},... | collective-permute-start | bytes 393224 | tf_op jit(solution)/shard_map/ppermute | solution.py:22
  11.2 21.4 %collective-permute-start.2 = (bf16[2,128,512]{2,1,0:T(8,128)(2,1)S(1)}, bf16[2,128,512]{2,1,0:T(8,128)(2,1)S(1)}, u32[]{:S(2)}, u32[]{:S(2)}) collective-permute-start(bf16[2,128,512]{2,1,0:T(8,128)(2,1)S(1)} %collective-permute-done.refs_0_), channel_id=1, source_target_pairs={{0,1},{1,0},{2,3},{3,2},{4,5},{5,4},{6,7},{7,6},{8,9},{9,8},{10,11... | collective-permute-start | bytes 786440 | tf_op jit(solution)/shard_map/ppermute | solution.py:26
  14.3 18.4 %collective-permute-start.3 = (bf16[2,128,512]{2,1,0:T(8,128)(2,1)S(1)}, bf16[2,128,512]{2,1,0:T(8,128)(2,1)S(1)}, u32[]{:S(2)}, u32[]{:S(2)}) collective-permute-start(bf16[2,128,512]{2,1,0:T(8,128)(2,1)S(1)} %collective-permute-done.1.refs_1_), channel_id=1, source_target_pairs={{0,1},{1,0},{2,3},{3,2},{4,5},{5,4},{6,7},{7,6},{8,9},{9,8},{10,11... | collective-permute-start | bytes 786440 | tf_op jit(solution)/shard_map/ppermute | solution.py:26
  16.8 15.3 %collective-permute-start.5 = (bf16[128,512]{1,0:T(8,128)(2,1)S(1)}, bf16[128,512]{1,0:T(8,128)(2,1)S(1)}, u32[]{:S(2)}, u32[]{:S(2)}) collective-permute-start(bf16[128,512]{1,0:T(8,128)(2,1)S(1)} %get-tuple-element.22), channel_id=1, source_target_pairs={{0,10},{1,15},{2,8},{3,13},{4,14},{5,11},{6,12},{7,9},{8,2},{9,7},... | collective-permute-start | bytes 393224 | tf_op jit(solution)/shard_map/ppermute | solution.py:22
  21.3 10.8 %collective-permute-start.13 = (bf16[128,512]{1,0:T(8,128)(2,1)S(1)}, bf16[128,512]{1,0:T(8,128)(2,1)S(1)}, u32[]{:S(2)}, u32[]{:S(2)}) collective-permute-start(bf16[128,512]{1,0:T(8,128)(2,1)S(1)} %collective-permute-done.11.refs_4_), channel_id=1, source_target_pairs={{0,1},{1,0},{2,3},{3,2},{4,5},{5,4},{6,7},{7,6},{8,9},{9,8},{10,11... | collective-permute-start | bytes 393224 | tf_op jit(solution)/shard_map/ppermute | solution.py:26
  28.9 3.7 %collective-permute-start.14 = (bf16[128,512]{1,0:T(8,128)(2,1)S(1)}, bf16[128,512]{1,0:T(8,128)(2,1)S(1)}, u32[]{:S(2)}, u32[]{:S(2)}) collective-permute-start(bf16[128,512]{1,0:T(8,128)(2,1)S(1)} %collective-permute-done.12.refs_5_), channel_id=1, source_target_pairs={{0,1},{1,0},{2,3},{3,2},{4,5},{5,4},{6,7},{7,6},{8,9},{9,8},{10,11... | collective-permute-start | bytes 393224 | tf_op jit(solution)/shard_map/ppermute | solution.py:26
  32.1 5.0 %collective-permute-start.6 = (bf16[128,512]{1,0:T(8,128)(2,1)S(1)}, bf16[128,512]{1,0:T(8,128)(2,1)S(1)}, u32[]{:S(2)}, u32[]{:S(2)}) collective-permute-start(bf16[128,512]{1,0:T(8,128)(2,1)S(1)} %collective-permute-done.4.refs_4_), channel_id=1, source_target_pairs={{0,1},{1,0},{2,3},{3,2},{4,5},{5,4},{6,7},{7,6},{8,9},{9,8},{10,11... | collective-permute-start | bytes 393224 | tf_op jit(solution)/shard_map/ppermute | solution.py:26
  32.1 5.0 %collective-permute-start.7 = (bf16[128,512]{1,0:T(8,128)(2,1)S(1)}, bf16[128,512]{1,0:T(8,128)(2,1)S(1)}, u32[]{:S(2)}, u32[]{:S(2)}) collective-permute-start(bf16[128,512]{1,0:T(8,128)(2,1)S(1)} %collective-permute-done.5.refs_5_), channel_id=1, source_target_pairs={{0,1},{1,0},{2,3},{3,2},{4,5},{5,4},{6,7},{7,6},{8,9},{9,8},{10,11... | collective-permute-start | bytes 393224 | tf_op jit(solution)/shard_map/ppermute | solution.py:26
  33.5 7.3 %collective-permute-start.15 = (bf16[128,512]{1,0:T(8,128)(2,1)S(1)}, bf16[128,512]{1,0:T(8,128)(2,1)S(1)}, u32[]{:S(2)}, u32[]{:S(2)}) collective-permute-start(bf16[128,512]{1,0:T(8,128)(2,1)S(1)} %get-tuple-element.30), channel_id=1, source_target_pairs={{0,2},{1,3},{2,0},{3,1},{4,6},{5,7},{6,4},{7,5},{8,10},{9,11},{10,... | collective-permute-start | bytes 393224 | tf_op jit(solution)/shard_map/ppermute | solution.py:22
  34.7 6.9 %collective-permute-start.16 = (bf16[128,512]{1,0:T(8,128)(2,1)S(1)}, bf16[128,512]{1,0:T(8,128)(2,1)S(1)}, u32[]{:S(2)}, u32[]{:S(2)}) collective-permute-start(bf16[128,512]{1,0:T(8,128)(2,1)S(1)} %get-tuple-element.31), channel_id=1, source_target_pairs={{0,4},{1,5},{2,6},{3,7},{4,0},{5,1},{6,2},{7,3},{8,12},{9,13},{10,... | collective-permute-start | bytes 393224 | tf_op jit(solution)/shard_map/ppermute | solution.py:22
  35.6 8.7 %collective-permute-start.17 = (bf16[128,512]{1,0:T(8,128)(2,1)S(1)}, bf16[128,512]{1,0:T(8,128)(2,1)S(1)}, u32[]{:S(2)}, u32[]{:S(2)}) collective-permute-start(bf16[128,512]{1,0:T(8,128)(2,1)S(1)} %get-tuple-element.32), channel_id=1, source_target_pairs={{0,6},{1,7},{2,4},{3,5},{4,2},{5,3},{6,0},{7,1},{8,14},{9,15},{10,... | collective-permute-start | bytes 393224 | tf_op jit(solution)/shard_map/ppermute | solution.py:22
  38.0 9.1 %collective-permute-start.10 = (bf16[128,512]{1,0:T(8,128)(2,1)S(1)}, bf16[128,512]{1,0:T(8,128)(2,1)S(1)}, u32[]{:S(2)}, u32[]{:S(2)}) collective-permute-start(bf16[128,512]{1,0:T(8,128)(2,1)S(1)} %get-tuple-element.26), channel_id=1, source_target_pairs={{0,6},{1,7},{2,4},{3,5},{4,2},{5,3},{6,0},{7,1},{8,14},{9,15},{10,... | collective-permute-start | bytes 393224 | tf_op jit(solution)/shard_map/ppermute | solution.py:22
  39.4 9.2 %collective-permute-start.8 = (bf16[128,512]{1,0:T(8,128)(2,1)S(1)}, bf16[128,512]{1,0:T(8,128)(2,1)S(1)}, u32[]{:S(2)}, u32[]{:S(2)}) collective-permute-start(bf16[128,512]{1,0:T(8,128)(2,1)S(1)} %get-tuple-element.24), channel_id=1, source_target_pairs={{0,2},{1,3},{2,0},{3,1},{4,6},{5,7},{6,4},{7,5},{8,10},{9,11},{10,... | collective-permute-start | bytes 393224 | tf_op jit(solution)/shard_map/ppermute | solution.py:22
  40.8 7.8 %collective-permute-start.9 = (bf16[128,512]{1,0:T(8,128)(2,1)S(1)}, bf16[128,512]{1,0:T(8,128)(2,1)S(1)}, u32[]{:S(2)}, u32[]{:S(2)}) collective-permute-start(bf16[128,512]{1,0:T(8,128)(2,1)S(1)} %get-tuple-element.25), channel_id=1, source_target_pairs={{0,4},{1,5},{2,6},{3,7},{4,0},{5,1},{6,2},{7,3},{8,12},{9,13},{10,... | collective-permute-start | bytes 393224 | tf_op jit(solution)/shard_map/ppermute | solution.py:22
  48.6 0.7 %copy-start.1 = (s32[32]{0:T(128)S(1)}, s32[32]{0:T(128)}, u32[]{:S(2)}) copy-start(s32[32]{0:T(128)} %table.1) | copy-start | bytes 388
